TPU v7x, 128 devices: a whole 4x4x4 slice. The times are simulated.
128 devices in a mesh: row: 8 (over x, core), col: 16 (over y, z).
Axes of the slice: x: 4, y: 4, z: 4, core: 2. Of those that a mesh axis runs over, the one named last changes fastest.
Arguments:
- right_side: float32 [131072, 128], P(('row', 'col')), may hold values from -6 to 6
- leaf_inverse: bfloat16 [131072, 1024], P(('row', 'col')), may hold values from -0.1875 to 0.1875
- compress: bfloat16 [131072, 2048], P(('row', 'col')), may hold values from -0.1875 to 0.1875
- middle: bfloat16 [262144, 2048], P(('row', 'col')), may hold values from -0.125 to 0.125
- expand: bfloat16 [131072, 2048], P(('row', 'col')), may hold values from -0.125 to 0.125
- row_project: bfloat16 [3, 131072, 256], P(None, ('row', 'col')), may hold values from -0.1875 to 0.1875
- row_expand: bfloat16 [3, 131072, 256], P(None, ('row', 'col')), may hold values from -0.25 to 0.25
- root_project: bfloat16 [131072, 256], P(('row', 'col')), may hold values from -0.015625 to 0.015625
- root_expand: bfloat16 [131072, 256], P(('row', 'col')), may hold values from -0.375 to 0.375
- owner_map: int32 [16], replicated, may hold values from 0 to 15, each once
Outputs:
- applied: float32 [131072, 128], P(('row', 'col'))
Inputs may be any that keep to these rules, and one draw needn't show every extreme that they name: owner_map names each of the 16 column positions exactly once.
All inputs are finite; a program needn't handle non-finite values.
Results may differ from a plain program's by a relative error of at most 0.004.
Values may be sent and summed in bfloat16 or wider, within the bound.
A program may use at most 128 MiB of HBM per device.

v0:
```python
import jax
import jax.numpy as jnp
from jax import lax
from jax.sharding import PartitionSpec as P

contract_first = (((0,), (0,)), ((), ()))


def swapped(x, axis, bit):
    return lax.ppermute(x, axis, [(i, i ^ 1 << bit) for i in range(lax.axis_size(axis))])


def per_device(
    right_side,
    leaf_inverse,
    compress,
    middle,
    expand,
    row_project,
    row_expand,
    root_project,
    root_expand,
    owner_map,
):
    lowered = right_side.astype(jnp.bfloat16)
    columns = lowered.shape[1]
    dense_part = jnp.dot(leaf_inverse, lowered, preferred_element_type=jnp.float32)
    coeffs = lax.dot_general(
        compress, lowered, contract_first, preferred_element_type=jnp.float32
    ).astype(jnp.bfloat16)
    col_count = lax.axis_size("col")
    pieces = coeffs.reshape(col_count, -1, columns)
    inverse = jnp.argsort(owner_map)
    outgoing = jnp.take(pieces, inverse, axis=0)
    arrived = lax.all_to_all(outgoing, "col", split_axis=0, concat_axis=0, tiled=True)
    shape_now = arrived.shape
    mixed_rows = jnp.dot(
        middle, arrived.reshape(-1, shape_now[2]), preferred_element_type=jnp.float32
    )
    mixed_rows = mixed_rows.astype(jnp.bfloat16).reshape(shape_now)
    returned = lax.all_to_all(mixed_rows, "col", split_axis=0, concat_axis=0, tiled=True)
    ordered = jnp.take(returned, owner_map, axis=0).reshape(-1, columns)
    cluster_part = jnp.dot(expand, ordered, preferred_element_type=jnp.float32)
    level_coeffs = jnp.einsum(
        "blr,lw->brw", row_project, lowered, preferred_element_type=jnp.float32
    )
    root_term = lax.dot_general(
        root_project, lowered, contract_first, preferred_element_type=jnp.float32
    )
    levels = lax.axis_size("row").bit_length() - 1
    running = level_coeffs
    siblings = []
    for level_bit in range(levels):
        partner = swapped(running[level_bit:], "row", level_bit)
        siblings.append(partner[0])
        running = jnp.concatenate(
            [running[: level_bit + 1], running[level_bit + 1 :] + partner[1:]], axis=0
        )
    sibling_sum = jnp.stack(siblings, axis=0)
    root_sum = jnp.sum(lax.all_gather(lax.psum(root_term, "row"), "col", axis=0), axis=0)
    coupled = jnp.einsum(
        "blr,brw->lw",
        row_expand,
        sibling_sum.astype(jnp.bfloat16),
        preferred_element_type=jnp.float32,
    )
    root_part = jnp.dot(
        root_expand, root_sum.astype(jnp.bfloat16), preferred_element_type=jnp.float32
    )
    return dense_part + cluster_part + coupled + root_part


def solution(mesh):
    in_specs = (
        P(("row", "col"), None),
        P(("row", "col"), None),
        P(("row", "col"), None),
        P(("row", "col"), None),
        P(("row", "col"), None),
        P(None, ("row", "col"), None),
        P(None, ("row", "col"), None),
        P(("row", "col"), None),
        P(("row", "col"), None),
        P(),
    )
    out_specs = P(("row", "col"), None)
    return jax.shard_map(
        per_device, mesh=mesh, in_specs=in_specs, out_specs=out_specs, check_vma=False
    )
```

profile of v0, /device:TPU:6, one launch (start us, length us, event | category | flops | bytes accessed | tf_op | source)
XLA Modules:
  0.0 139.6 jit_solution(6744168782270515428)
XLA Ops:
  6.5 0.0 copy-start
  6.5 0.0 all-reduce.2.cloned.1.call-start
  6.5 1.2 convert_element_type.16
  7.8 2.0 %convolution_bitcast_fusion.3 = f32[1,256,128]{2,1,0:T(8,128)} fusion(bf16[1024,256]{1,0:T(8,128)(2,1)} %param.19, bf16[1024,128]{1,0:T(8,128)(2,1)S(1)} %convert_element_type.16), kind=kOutput, calls=%fused_computation.11 | convolution fusion | flops 67108864 | bytes 917504 | tf_op jit(solution)/shard_map/dot_general | solution.py:47
  9.8 0.0 all-reduce.2.cloned.1.call-update
  9.8 0.0 all-gather.2.cloned.1.call-start
  9.9 1.9 %sort.17 = (s32[16]{0:T(128)}, s32[16]{0:T(128)S(1)}) sort(s32[16]{0:T(128)} %param.21, s32[16]{0:T(128)S(1)} %iota.4), dimensions={0}, to_apply=%region_0.0 | sort | flops 64 | bytes 256 | tf_op jit(solution)/shard_map/jit(argsort)/sort | solution.py:33
  11.8 57.5 %all-reduce.2.cloned.1.call-done = f32[1,256,128]{2,1,0:T(8,128)} async-done(((f32[1,256,128]{2,1,0:T(8,128)}), f32[1,256,128]{2,1,0:T(8,128)}) %all-reduce.2.cloned.1.call-update) | async-done | bytes 131088 | tf_op jit(solution)/shard_map/psum | solution.py:60
  69.2 0.0 all-gather.2.cloned.1.call-update
  69.3 3.5 %convolution_convert_fusion.1 = bf16[2048,128]{1,0:T(8,128)(2,1)S(1)} fusion(bf16[1024,2048]{1,0:T(8,128)(2,1)} %param.14, bf16[1024,128]{1,0:T(8,128)(2,1)S(1)} %convert_element_type.16), kind=kOutput, calls=%fused_computation.3 | convolution fusion | flops 537133056 | bytes 4980736 | tf_op jit(solution)/shard_map/dot_general | solution.py:28
  72.8 0.6 gather_fusion
  73.5 0.9 broadcast_select_fusion.1
  74.4 7.0 %all-to-all-start = ((bf16[16,128,128]{2,1,0:T(8,128)(2,1)}), bf16[16,128,128]{2,1,0:T(8,128)(2,1)}, u32[]{:S(2)}, u32[]{:S(2)}) async-start(bf16[16,128,128]{2,1,0:T(8,128)(2,1)} %broadcast_select_fusion.1), calls=%async_computation | async-start | bytes 1048576 | tf_op jit(solution)/shard_map/all_to_all | solution.py:35
  81.4 0.0 copy-start.3
  81.4 2.1 %fusion.4 = f32[3,256,128]{2,1,0:T(8,128)S(1)} fusion(bf16[3,1024,256]{2,1,0:T(8,128)(2,1)} %param.17, bf16[1024,128]{1,0:T(8,128)(2,1)S(1)} %convert_element_type.16), kind=kOutput, calls=%fused_computation.15 | convolution fusion | flops 201326592 | bytes 2228224 | tf_op jit(solution)/shard_map/blr,lw->brw/dot_general | solution.py:44
  83.5 0.4 collective-permute-start
  83.9 0.0 copy-done
  83.9 0.7 fusion.14
  84.6 0.0 copy-done.3
  84.7 0.6 collective-permute-done
  85.3 0.0 copy-start.2
  85.3 0.7 copy-done.2
  86.0 0.0 collective-permute-start.1
  86.1 9.2 %all-to-all-done = bf16[16,128,128]{2,1,0:T(8,128)(2,1)} async-done(((bf16[16,128,128]{2,1,0:T(8,128)(2,1)}), bf16[16,128,128]{2,1,0:T(8,128)(2,1)}, u32[]{:S(2)}, u32[]{:S(2)}) %all-to-all-start) | async-done | bytes 524320 | tf_op jit(solution)/shard_map/all_to_all | solution.py:35
  95.3 6.5 %fusion = bf16[2048,128]{0,1:T(8,128)(2,1)S(1)} fusion(bf16[2048,128]{1,0:T(8,128)(2,1)} %bitcast.1, bf16[2048,2048]{1,0:T(8,128)(2,1)} %param.15), kind=kOutput, calls=%fused_computation.4 | convolution fusion | flops 1074003968 | bytes 9437184 | tf_op jit(solution)/shard_map/dot_general | solution.py:37
  101.8 1.0 copy.33
  102.8 3.6 %all-to-all-start.1 = ((bf16[16,128,128]{2,1,0:T(8,128)(2,1)}), bf16[16,128,128]{2,1,0:T(8,128)(2,1)S(1)}, u32[]{:S(2)}, u32[]{:S(2)}) async-start(bf16[16,128,128]{2,1,0:T(8,128)(2,1)} %bitcast.40), calls=%async_computation.1 | async-start | bytes 1048576 | tf_op jit(solution)/shard_map/all_to_all | solution.py:41
  106.4 0.9 slice.43
  107.3 0.0 collective-permute-done.1
  107.3 1.6 %fusion.13 = (bf16[1,256,128]{2,1,0:T(8,128)(2,1)S(1)}, bf16[1,256,128]{2,1,0:T(8,128)(2,1)}) fusion(f32[2,256,128]{2,1,0:T(8,128)} %collective-permute-done.1, f32[2,256,128]{2,1,0:T(8,128)S(1)} %slice_add_fusion), kind=kLoop, calls=%fused_computation.33 | loop fusion | flops 65536 | bytes 458752 | tf_op jit(solution)/shard_map/slice | solution.py:55
  108.9 0.0 collective-permute-start.2
  108.9 13.0 %all-to-all-done.1 = bf16[16,128,128]{2,1,0:T(8,128)(2,1)S(1)} async-done(((bf16[16,128,128]{2,1,0:T(8,128)(2,1)}), bf16[16,128,128]{2,1,0:T(8,128)(2,1)S(1)}, u32[]{:S(2)}, u32[]{:S(2)}) %all-to-all-start.1) | async-done | bytes 524320 | tf_op jit(solution)/shard_map/all_to_all | solution.py:41
  121.9 1.4 %gather_fusion.1 = bf16[16,128,128]{2,1,0:T(8,128)(2,1)} fusion(bf16[16,128,128]{2,1,0:T(8,128)(2,1)S(1)} %all-to-all-done.1, s32[1024]{0:T(1024)S(1)} %pad_clamp_fusion), kind=kCustom, calls=%fused_computation.1.clone | custom fusion | bytes 1048640 | tf_op jit(solution)/shard_map/jit(_take)/gather | solution.py:42
  123.3 1.2 broadcast_select_fusion
  124.5 3.5 %fusion.1 = f32[1024,128]{1,0:T(8,128)S(1)} fusion(f32[1024,128]{1,0:T(8,128)S(1)} %fusion.14, bf16[1024,2048]{1,0:T(8,128)(2,1)} %param.16, bf16[2048,128]{1,0:T(8,128)(2,1)S(1)} %bitcast.39), kind=kOutput, calls=%fused_computation.8 | convolution fusion | flops 537001984 | bytes 5767168 | tf_op jit(solution)/shard_map/dot_general | solution.py:43
  127.9 0.0 copy-start.1
  127.9 0.0 all-gather.2.cloned.1.call-done
  128.0 1.7 %reduce_sum.9 = bf16[256,128]{1,0:T(8,128)(2,1)S(1)} reduce(f32[16,256,128]{2,1,0:T(8,128)} %all-gather.2.cloned.1.call-done, f32[]{:T(128)} %constant.1.clone.1), dimensions={0}, to_apply=%region_2.4 | reduce | flops 491520 | bytes 2162692 | tf_op jit(solution)/shard_map/reduce_sum | solution.py:60
  129.7 0.0 copy-done.1
  129.7 0.3 convolution_bitcast_fusion
  130.0 0.0 collective-permute-done.2
  130.0 2.8 %fusion.3 = f32[1024,128]{1,0:T(8,128)} fusion(f32[1024,128]{1,0:T(8,128)S(1)} %convolution_bitcast_fusion, f32[1024,128]{1,0:T(8,128)S(1)} %fusion.1, bf16[3,1024,256]{2,1,0:T(8,128)(2,1)} %param.18, bf16[1,256,128]{2,1,0:T(8,128)(2,1)} %collective-permute-done.2, bf16[1,256,128]{2,1,0:T(8,128)(2,1)S(1)} %get-tuple-element.8, ...), kind=kOutput, calls=%fused_computation.10 | convolution fusion | flops 201785344 | bytes 3342336 | tf_op jit(solution)/shard_map/blr,brw->lw/dot_general | solution.py:61
  (8 shorter events, 0.1 us)
Async XLA Ops:
  6.5 77.4 %copy-start = (bf16[1024,1024]{1,0:T(8,128)(2,1)S(1)}, bf16[1024,1024]{1,0:T(8,128)(2,1)}, u32[]{:S(2)}) copy-start(bf16[1024,1024]{1,0:T(8,128)(2,1)} %param.13) | copy-start | bytes 6291460
  6.5 62.7 %all-reduce.2.cloned.1.call-start = ((), (), s32[]{:S(2)}) async-start(), calls=%async_computation.2 | async-start | bytes 262144 | tf_op jit(solution)/shard_map/psum | solution.py:60
  9.8 118.1 %all-gather.2.cloned.1.call-start = ((), (), s32[]{:S(2)}) async-start(), calls=%async_computation.3 | async-start | bytes 2228224 | tf_op jit(solution)/shard_map/all_gather | solution.py:60
  74.4 20.9 %all-to-all-start = ((bf16[16,128,128]{2,1,0:T(8,128)(2,1)}), bf16[16,128,128]{2,1,0:T(8,128)(2,1)}, u32[]{:S(2)}, u32[]{:S(2)}) async-start(bf16[16,128,128]{2,1,0:T(8,128)(2,1)} %broadcast_select_fusion.1), calls=%async_computation | async-start | bytes 1048576 | tf_op jit(solution)/shard_map/all_to_all | solution.py:35
  81.4 3.2 %copy-start.3 = (s32[16]{0:T(128)S(1)}, s32[16]{0:T(128)}, u32[]{:S(2)}) copy-start(s32[16]{0:T(128)} %param.21) | copy-start | bytes 196
  83.5 1.8 %collective-permute-start = (f32[3,256,128]{2,1,0:T(8,128)S(1)}, f32[3,256,128]{2,1,0:T(8,128)S(1)}, u32[]{:S(2)}, u32[]{:S(2)}) collective-permute-start(f32[3,256,128]{2,1,0:T(8,128)S(1)} %fusion.4), channel_id=1, source_target_pairs={{0,16},{16,0},{32,48},{48,32},{64,80},{80,64},{96,112},{112,96},{1... | collective-permute-start | bytes 1179656 | tf_op jit(solution)/shard_map/ppermute | solution.py:10
  85.3 0.8 copy-start.2
  86.0 21.2 %collective-permute-start.1 = (f32[2,256,128]{2,1,0:T(8,128)S(1)}, f32[2,256,128]{2,1,0:T(8,128)}, u32[]{:S(2)}, u32[]{:S(2)}) collective-permute-start(f32[2,256,128]{2,1,0:T(8,128)S(1)} %slice_add_fusion), channel_id=1, source_target_pairs={{0,32},{16,48},{32,0},{48,16},{64,96},{80,112},{96,64},{112,80},{1... | collective-permute-start | bytes 786440 | tf_op jit(solution)/shard_map/ppermute | solution.py:10
  102.8 19.1 %all-to-all-start.1 = ((bf16[16,128,128]{2,1,0:T(8,128)(2,1)}), bf16[16,128,128]{2,1,0:T(8,128)(2,1)S(1)}, u32[]{:S(2)}, u32[]{:S(2)}) async-start(bf16[16,128,128]{2,1,0:T(8,128)(2,1)} %bitcast.40), calls=%async_computation.1 | async-start | bytes 1048576 | tf_op jit(solution)/shard_map/all_to_all | solution.py:41
  108.9 21.1 %collective-permute-start.2 = (bf16[1,256,128]{2,1,0:T(8,128)(2,1)}, bf16[1,256,128]{2,1,0:T(8,128)(2,1)}, u32[]{:S(2)}, u32[]{:S(2)}) collective-permute-start(bf16[1,256,128]{2,1,0:T(8,128)(2,1)} %get-tuple-element.9), channel_id=1, source_target_pairs={{0,64},{16,80},{32,96},{48,112},{64,0},{80,16},{96,32},{112,48},{1... | collective-permute-start | bytes 196616 | tf_op jit(solution)/shard_map/ppermute | solution.py:10
  127.9 1.8 %copy-start.1 = (bf16[1024,256]{1,0:T(8,128)(2,1)S(1)}, bf16[1024,256]{1,0:T(8,128)(2,1)}, u32[]{:S(2)}) copy-start(bf16[1024,256]{1,0:T(8,128)(2,1)} %param.20) | copy-start | bytes 1572868
Sparse Core Ops, SparseCore 0:
  9.9 59.2 all-reduce.1
  71.6 53.5 all-gather.1
where the time goes:
time: 140 us
  waiting for transfers between devices  80.3 us (57%)
  matrix products  21.3 us (15%)
  between operations  13.6 us (10%)
  starting transfers between devices  11.1 us (8%)
  other arithmetic  8.62 us (6%)
  local copies, waits for them, and re-layouts  4.72 us (3%)
    psum x1, waiting for transfers between devices, per_device(): lax.psum(root_term, 'row')  57.5 us
    all_to_all x1, waiting for transfers between devices, per_device(): lax.all_to_all(mixed_rows, 'col', split_axis=0, concat_axis=0, tiled=True)  13 us
    all_to_all x1, waiting for transfers between devices, per_device(): lax.all_to_all(outgoing, 'col', split_axis=0, concat_axis=0, tiled=True)  9.2 us
    all_to_all x1, starting transfers between devices, per_device(): lax.all_to_all(outgoing, 'col', split_axis=0, concat_axis=0, tiled=True)  7.03 us
    dot_general x1, matrix products, per_device(): jnp.dot(middle, arrived.reshape(-1, shape_now[2]), preferred_element_type...  6.49 us
    all_to_all x1, starting transfers between devices, per_device(): lax.all_to_all(mixed_rows, 'col', split_axis=0, concat_axis=0, tiled=True)  3.57 us
    dot_general x1, matrix products, per_device(): lax.dot_general(compress, lowered, contract_first, preferred_element_type...  3.5 us
    dot_general x1, matrix products, per_device(): cluster_part = jnp.dot(expand, ordered, preferred_element_type=jnp.float32)  3.45 us
  transfers between devices with their start and end apart: 7, of which 4 were waited for; matrix products, arithmetic and copies ran while one was open for 20% of the time, Pallas kernels for 0%

commit v1 on v0

--- a/solution.py
+++ b/solution.py
@@ -4,6 +4,12 @@
 from jax.sharding import PartitionSpec as P
 
 contract_first = (((0,), (0,)), ((), ()))
+
+
+def add_all(x, axis):
+    parts = lax.all_gather(x, axis, axis=0, tiled=False)
+    acc = parts.sum(axis=0)
+    return acc
 
 
 def swapped(x, axis, bit):
@@ -57,7 +63,7 @@
             [running[: level_bit + 1], running[level_bit + 1 :] + partner[1:]], axis=0
         )
     sibling_sum = jnp.stack(siblings, axis=0)
-    root_sum = jnp.sum(lax.all_gather(lax.psum(root_term, "row"), "col", axis=0), axis=0)
+    root_sum = jnp.sum(lax.all_gather(add_all(root_term, "row"), "col", axis=0), axis=0)
     coupled = jnp.einsum(
         "blr,brw->lw",
         row_expand,

time: 140 us -> 108 us (0.77); the launches traced: 140 us -> 106 us
  waiting for transfers between devices: 80.3 us -> 42.4 us
  starting transfers between devices: 11.1 us -> 13.3 us
  other arithmetic: 8.62 us -> 10.6 us
    psum x1 -> x0, waiting for transfers between devices: 57.5 us -> none  [per_device(): lax.psum(root_term, 'row')]
    all_gather x1 -> x2, waiting for transfers between devices: 0.02 us -> 22.1 us  [the longest x1 22.1 us: add_all(): parts = lax.all_gather(x, axis, axis=0, tiled=False)]
    ppermute x3, starting transfers between devices: 0.45 us -> 2.68 us  [swapped(): lax.ppermute(x, axis, [(i, i ^ 1 << bit) for i in range(lax.axis_size(axi...]
    reduce_sum x1 -> x2, other arithmetic: 1.75 us -> 3.69 us  [the longest x1 1.94 us: add_all(): acc = parts.sum(axis=0)]
    all_to_all x1, waiting for transfers between devices: 13 us -> 11.5 us  [per_device(): lax.all_to_all(mixed_rows, 'col', split_axis=0, concat_axis=0, tiled=True)]
  transfers between devices with their start and end apart: 7 -> 7, of which waited for: 4 -> 4; matrix products, arithmetic and copies ran while one was open for 20% -> 26% of each run, Pallas kernels for 0% -> 0%
where the time goes in v1:
time: 108 us; the launch traced here: 106 us
  waiting for transfers between devices  42.4 us (39%)
  matrix products  21.3 us (20%)
  between operations  13.6 us (13%)
  starting transfers between devices  13.3 us (12%)
  other arithmetic  10.6 us (10%)
  local copies, waits for them, and re-layouts  4.72 us (4%)
    all_gather x1, waiting for transfers between devices, add_all(): parts = lax.all_gather(x, axis, axis=0, tiled=False)  22.1 us
    all_to_all x1, waiting for transfers between devices, per_device(): lax.all_to_all(mixed_rows, 'col', split_axis=0, concat_axis=0, tiled=True)  11.5 us
    all_to_all x1, waiting for transfers between devices, per_device(): lax.all_to_all(outgoing, 'col', split_axis=0, concat_axis=0, tiled=True)  7.84 us
    all_to_all x1, starting transfers between devices, per_device(): lax.all_to_all(outgoing, 'col', split_axis=0, concat_axis=0, tiled=True)  7.03 us
    dot_general x1, matrix products, per_device(): jnp.dot(middle, arrived.reshape(-1, shape_now[2]), preferred_element_type...  6.48 us
    all_to_all x1, starting transfers between devices, per_device(): lax.all_to_all(mixed_rows, 'col', split_axis=0, concat_axis=0, tiled=True)  3.59 us
    dot_general x1, matrix products, per_device(): lax.dot_general(compress, lowered, contract_first, preferred_element_type...  3.5 us
    dot_general x1, matrix products, per_device(): cluster_part = jnp.dot(expand, ordered, preferred_element_type=jnp.float32)  3.45 us
  transfers between devices with their start and end apart: 7, of which 4 were waited for; matrix products, arithmetic and copies ran while one was open for 26% of the time, Pallas kernels for 0%

profile of v1, /device:TPU:6, one launch (start us, length us, event | category | flops | bytes accessed | tf_op | source)
XLA Modules:
  0.0 106.0 jit_solution(2589416082276399458)
XLA Ops:
  6.5 0.0 copy-start
  6.5 0.0 all-gather.5.cloned.1.call-start
  6.5 1.2 %convert_element_type.16 = bf16[1024,128]{1,0:T(8,128)(2,1)S(1)} convert(f32[1024,128]{1,0:T(8,128)} %param.12) | non-fusion elementwise | flops 131072 | bytes 786432 | tf_op jit(solution)/shard_map/convert_element_type | solution.py:31
  7.8 2.0 %fusion.15 = f32[256,128]{1,0:T(8,128)} fusion(bf16[1024,256]{1,0:T(8,128)(2,1)} %param.19, bf16[1024,128]{1,0:T(8,128)(2,1)S(1)} %convert_element_type.16), kind=kOutput, calls=%fused_computation.34 | convolution fusion | flops 67108864 | bytes 917504 | tf_op jit(solution)/shard_map/dot_general | solution.py:53
  9.8 0.0 all-gather.5.cloned.1.call-update
  9.8 0.0 all-gather.7.cloned.1.call-start
  9.9 2.0 %sort.17 = (s32[16]{0:T(128)}, s32[16]{0:T(128)S(1)}) sort(s32[16]{0:T(128)} %param.21, s32[16]{0:T(128)S(1)} %iota.4), dimensions={0}, to_apply=%region_0.0 | sort | flops 64 | bytes 256 | tf_op jit(solution)/shard_map/jit(argsort)/sort | solution.py:39
  11.8 22.1 %all-gather.5.cloned.1.call-done = f32[2048,128]{1,0:T(8,128)} async-done(((f32[256,128]{1,0:T(8,128)}), f32[2048,128]{1,0:T(8,128)}) %all-gather.5.cloned.1.call-update) | async-done | bytes 1048592 | tf_op jit(solution)/shard_map/all_gather | solution.py:10
  34.0 1.9 %reduce_sum.18 = f32[256,128]{1,0:T(8,128)} reduce(f32[8,256,128]{2,1,0:T(8,128)} %bitcast.42, f32[]{:T(128)} %constant.1.clone.1), dimensions={0}, to_apply=%region_1.3 | reduce | flops 229376 | bytes 1179652 | tf_op jit(solution)/shard_map/reduce_sum | solution.py:11
  35.9 0.0 all-gather.7.cloned.1.call-update
  36.0 3.5 %convolution_convert_fusion.1 = bf16[2048,128]{1,0:T(8,128)(2,1)S(1)} fusion(bf16[1024,2048]{1,0:T(8,128)(2,1)} %param.14, bf16[1024,128]{1,0:T(8,128)(2,1)S(1)} %convert_element_type.16), kind=kOutput, calls=%fused_computation.3 | convolution fusion | flops 537133056 | bytes 4980736 | tf_op jit(solution)/shard_map/dot_general | solution.py:34
  39.5 0.6 gather_fusion
  40.1 0.9 broadcast_select_fusion.1
  41.0 7.0 %all-to-all-start = ((bf16[16,128,128]{2,1,0:T(8,128)(2,1)}), bf16[16,128,128]{2,1,0:T(8,128)(2,1)}, u32[]{:S(2)}, u32[]{:S(2)}) async-start(bf16[16,128,128]{2,1,0:T(8,128)(2,1)} %broadcast_select_fusion.1), calls=%async_computation | async-start | bytes 1048576 | tf_op jit(solution)/shard_map/all_to_all | solution.py:41
  48.1 0.0 copy-start.3
  48.1 2.0 %fusion.4 = f32[3,256,128]{2,1,0:T(8,128)S(1)} fusion(bf16[3,1024,256]{2,1,0:T(8,128)(2,1)} %param.17, bf16[1024,128]{1,0:T(8,128)(2,1)S(1)} %convert_element_type.16), kind=kOutput, calls=%fused_computation.14 | convolution fusion | flops 201326592 | bytes 2228224 | tf_op jit(solution)/shard_map/blr,lw->brw/dot_general | solution.py:50
  50.1 0.1 collective-permute-start
  50.2 0.0 copy-done
  50.2 0.7 fusion.14
  50.9 0.0 copy-done.3
  51.0 1.0 collective-permute-done
  51.9 0.0 copy-start.2
  52.0 0.7 copy-done.2
  52.7 1.1 %collective-permute-start.1 = (f32[2,256,128]{2,1,0:T(8,128)S(1)}, f32[2,256,128]{2,1,0:T(8,128)}, u32[]{:S(2)}, u32[]{:S(2)}) collective-permute-start(f32[2,256,128]{2,1,0:T(8,128)S(1)} %slice_add_fusion), channel_id=1, source_target_pairs={{0,32},{16,48},{32,0},{48,16},{64,96},{80,112},{96,64},{112,80},{1... | collective-permute-start | bytes 786440 | tf_op jit(solution)/shard_map/ppermute | solution.py:16
  53.8 7.8 %all-to-all-done = bf16[16,128,128]{2,1,0:T(8,128)(2,1)} async-done(((bf16[16,128,128]{2,1,0:T(8,128)(2,1)}), bf16[16,128,128]{2,1,0:T(8,128)(2,1)}, u32[]{:S(2)}, u32[]{:S(2)}) %all-to-all-start) | async-done | bytes 524320 | tf_op jit(solution)/shard_map/all_to_all | solution.py:41
  61.7 6.5 %fusion = bf16[2048,128]{0,1:T(8,128)(2,1)S(1)} fusion(bf16[2048,128]{1,0:T(8,128)(2,1)} %bitcast.1, bf16[2048,2048]{1,0:T(8,128)(2,1)} %param.15), kind=kOutput, calls=%fused_computation.4 | convolution fusion | flops 1074003968 | bytes 9437184 | tf_op jit(solution)/shard_map/dot_general | solution.py:43
  68.1 1.0 copy.33
  69.1 3.6 %all-to-all-start.1 = ((bf16[16,128,128]{2,1,0:T(8,128)(2,1)}), bf16[16,128,128]{2,1,0:T(8,128)(2,1)S(1)}, u32[]{:S(2)}, u32[]{:S(2)}) async-start(bf16[16,128,128]{2,1,0:T(8,128)(2,1)} %bitcast.41), calls=%async_computation.1 | async-start | bytes 1048576 | tf_op jit(solution)/shard_map/all_to_all | solution.py:47
  72.8 0.9 slice.43
  73.7 0.0 collective-permute-done.1
  73.7 1.6 %fusion.13 = (bf16[1,256,128]{2,1,0:T(8,128)(2,1)S(1)}, bf16[1,256,128]{2,1,0:T(8,128)(2,1)}) fusion(f32[2,256,128]{2,1,0:T(8,128)} %collective-permute-done.1, f32[2,256,128]{2,1,0:T(8,128)S(1)} %slice_add_fusion), kind=kLoop, calls=%fused_computation.32 | loop fusion | flops 65536 | bytes 458752 | tf_op jit(solution)/shard_map/slice | solution.py:61
  75.3 1.5 %collective-permute-start.2 = (bf16[1,256,128]{2,1,0:T(8,128)(2,1)}, bf16[1,256,128]{2,1,0:T(8,128)(2,1)}, u32[]{:S(2)}, u32[]{:S(2)}) collective-permute-start(bf16[1,256,128]{2,1,0:T(8,128)(2,1)} %get-tuple-element.9), channel_id=1, source_target_pairs={{0,64},{16,80},{32,96},{48,112},{64,0},{80,16},{96,32},{112,48},{1... | collective-permute-start | bytes 196616 | tf_op jit(solution)/shard_map/ppermute | solution.py:16
  76.8 11.5 %all-to-all-done.1 = bf16[16,128,128]{2,1,0:T(8,128)(2,1)S(1)} async-done(((bf16[16,128,128]{2,1,0:T(8,128)(2,1)}), bf16[16,128,128]{2,1,0:T(8,128)(2,1)S(1)}, u32[]{:S(2)}, u32[]{:S(2)}) %all-to-all-start.1) | async-done | bytes 524320 | tf_op jit(solution)/shard_map/all_to_all | solution.py:47
  88.2 1.4 %gather_fusion.1 = bf16[16,128,128]{2,1,0:T(8,128)(2,1)} fusion(bf16[16,128,128]{2,1,0:T(8,128)(2,1)S(1)} %all-to-all-done.1, s32[1024]{0:T(1024)S(1)} %pad_clamp_fusion), kind=kCustom, calls=%fused_computation.1.clone | custom fusion | bytes 1048640 | tf_op jit(solution)/shard_map/jit(_take)/gather | solution.py:48
  89.6 1.2 %broadcast_select_fusion = bf16[16,128,128]{2,1,0:T(8,128)(2,1)S(1)} fusion(bf16[16,128,128]{2,1,0:T(8,128)(2,1)} %gather_fusion.1, pred[16]{0:T(512)(128)(4,1)S(1)} %compare_and_fusion), kind=kLoop, calls=%fused_computation.11 | loop fusion | flops 262144 | bytes 1048592 | tf_op jit(solution)/shard_map/jit(_take)/select_n | solution.py:48
  90.8 3.5 %fusion.1 = f32[1024,128]{1,0:T(8,128)S(1)} fusion(f32[1024,128]{1,0:T(8,128)S(1)} %fusion.14, bf16[1024,2048]{1,0:T(8,128)(2,1)} %param.16, bf16[2048,128]{1,0:T(8,128)(2,1)S(1)} %bitcast.40), kind=kOutput, calls=%fused_computation.8 | convolution fusion | flops 537001984 | bytes 5767168 | tf_op jit(solution)/shard_map/dot_general | solution.py:49
  94.3 0.0 copy-start.1
  94.3 0.0 all-gather.7.cloned.1.call-done
  94.3 1.7 %reduce_sum.19 = bf16[256,128]{1,0:T(8,128)(2,1)S(1)} reduce(f32[16,256,128]{2,1,0:T(8,128)} %bitcast.39, f32[]{:T(128)} %constant.1.clone.1), dimensions={0}, to_apply=%region_2.4 | reduce | flops 491520 | bytes 2162692 | tf_op jit(solution)/shard_map/reduce_sum | solution.py:66
  96.1 0.0 copy-done.1
  96.1 0.3 convolution_bitcast_fusion
  96.4 0.0 collective-permute-done.2
  96.4 2.8 %fusion.3 = f32[1024,128]{1,0:T(8,128)} fusion(f32[1024,128]{1,0:T(8,128)S(1)} %convolution_bitcast_fusion, f32[1024,128]{1,0:T(8,128)S(1)} %fusion.1, bf16[3,1024,256]{2,1,0:T(8,128)(2,1)} %param.18, bf16[1,256,128]{2,1,0:T(8,128)(2,1)} %collective-permute-done.2, bf16[1,256,128]{2,1,0:T(8,128)(2,1)S(1)} %get-tuple-element.8, ...), kind=kOutput, calls=%fused_computation.10 | convolution fusion | flops 201785344 | bytes 3342336 | tf_op jit(solution)/shard_map/blr,brw->lw/dot_general | solution.py:67
  (8 shorter events, 0.1 us)
Async XLA Ops:
  6.5 43.7 %copy-start = (bf16[1024,1024]{1,0:T(8,128)(2,1)S(1)}, bf16[1024,1024]{1,0:T(8,128)(2,1)}, u32[]{:S(2)}) copy-start(bf16[1024,1024]{1,0:T(8,128)(2,1)} %param.13) | copy-start | bytes 6291460
  6.5 27.4 %all-gather.5.cloned.1.call-start = ((), (), s32[]{:S(2)}) async-start(), calls=%async_computation.2 | async-start | bytes 1179648 | tf_op jit(solution)/shard_map/all_gather | solution.py:10
  9.8 84.5 %all-gather.7.cloned.1.call-start = ((), (), s32[]{:S(2)}) async-start(), calls=%async_computation.3 | async-start | bytes 2228224 | tf_op jit(solution)/shard_map/all_gather | solution.py:66
  41.0 20.6 %all-to-all-start = ((bf16[16,128,128]{2,1,0:T(8,128)(2,1)}), bf16[16,128,128]{2,1,0:T(8,128)(2,1)}, u32[]{:S(2)}, u32[]{:S(2)}) async-start(bf16[16,128,128]{2,1,0:T(8,128)(2,1)} %broadcast_select_fusion.1), calls=%async_computation | async-start | bytes 1048576 | tf_op jit(solution)/shard_map/all_to_all | solution.py:41
  48.1 2.9 %copy-start.3 = (s32[16]{0:T(128)S(1)}, s32[16]{0:T(128)}, u32[]{:S(2)}) copy-start(s32[16]{0:T(128)} %param.21) | copy-start | bytes 196
  50.1 1.8 %collective-permute-start = (f32[3,256,128]{2,1,0:T(8,128)S(1)}, f32[3,256,128]{2,1,0:T(8,128)S(1)}, u32[]{:S(2)}, u32[]{:S(2)}) collective-permute-start(f32[3,256,128]{2,1,0:T(8,128)S(1)} %fusion.4), channel_id=1, source_target_pairs={{0,16},{16,0},{32,48},{48,32},{64,80},{80,64},{96,112},{112,96},{1... | collective-permute-start | bytes 1179656 | tf_op jit(solution)/shard_map/ppermute | solution.py:16
  51.9 0.8 copy-start.2
  52.7 21.0 %collective-permute-start.1 = (f32[2,256,128]{2,1,0:T(8,128)S(1)}, f32[2,256,128]{2,1,0:T(8,128)}, u32[]{:S(2)}, u32[]{:S(2)}) collective-permute-start(f32[2,256,128]{2,1,0:T(8,128)S(1)} %slice_add_fusion), channel_id=1, source_target_pairs={{0,32},{16,48},{32,0},{48,16},{64,96},{80,112},{96,64},{112,80},{1... | collective-permute-start | bytes 786440 | tf_op jit(solution)/shard_map/ppermute | solution.py:16
  69.1 19.1 %all-to-all-start.1 = ((bf16[16,128,128]{2,1,0:T(8,128)(2,1)}), bf16[16,128,128]{2,1,0:T(8,128)(2,1)S(1)}, u32[]{:S(2)}, u32[]{:S(2)}) async-start(bf16[16,128,128]{2,1,0:T(8,128)(2,1)} %bitcast.41), calls=%async_computation.1 | async-start | bytes 1048576 | tf_op jit(solution)/shard_map/all_to_all | solution.py:47
  75.3 21.0 %collective-permute-start.2 = (bf16[1,256,128]{2,1,0:T(8,128)(2,1)}, bf16[1,256,128]{2,1,0:T(8,128)(2,1)}, u32[]{:S(2)}, u32[]{:S(2)}) collective-permute-start(bf16[1,256,128]{2,1,0:T(8,128)(2,1)} %get-tuple-element.9), channel_id=1, source_target_pairs={{0,64},{16,80},{32,96},{48,112},{64,0},{80,16},{96,32},{112,48},{1... | collective-permute-start | bytes 196616 | tf_op jit(solution)/shard_map/ppermute | solution.py:16
  94.3 1.8 %copy-start.1 = (bf16[1024,256]{1,0:T(8,128)(2,1)S(1)}, bf16[1024,256]{1,0:T(8,128)(2,1)}, u32[]{:S(2)}) copy-start(bf16[1024,256]{1,0:T(8,128)(2,1)} %param.20) | copy-start | bytes 1572868
Sparse Core Ops, SparseCore 0:
  9.9 23.9 all-gather.4
  36.1 55.1 all-gather.6
